TPU v7x, 32 devices: a whole 2x2x4 slice. The times are simulated.
32 devices in a mesh: dp: 8 (over z, y), tensor: 4 (over x, core).
Axes of the slice: x: 2, y: 2, z: 4, core: 2. Of those that a mesh axis runs over, the one named last changes fastest.
Arguments:
- tokens: bfloat16 [16384, 768], P(('dp', 'tensor')), may hold values from -6 to 6
- cotangent: bfloat16 [16384, 768], P(('dp', 'tensor')), may hold values from -6 to 6
- segment_ids: int32 [8, 2048], P('dp'), may hold values from 0 to 7, never falling along the last dimension, each value on 1 to 512 neighbouring positions
- ln1_gain: bfloat16 [768], P('dp'), may hold values from 0.5 to 1.5
- ln1_bias: bfloat16 [768], P('dp'), may hold values from -3 to 3
- w_query: bfloat16 [768, 768], P('dp', 'tensor'), may hold values from -0.3125 to 0.3125
- query_bias: bfloat16 [768], P('dp'), may hold values from -3 to 3
- w_key: bfloat16 [768, 768], P('dp', 'tensor'), may hold values from -0.3125 to 0.3125
- w_value: bfloat16 [768, 768], P('dp', 'tensor'), may hold values from -0.21875 to 0.21875
- value_bias: bfloat16 [768], P('dp'), may hold values from -3 to 3
- w_out: bfloat16 [768, 768], P('tensor', 'dp'), may hold values from -0.625 to 0.625
- out_bias: bfloat16 [768], P('dp'), may hold values from -3 to 3
- ln2_gain: bfloat16 [768], P('dp'), may hold values from 0.5 to 1.5
- ln2_bias: bfloat16 [768], P('dp'), may hold values from -3 to 3
- w_in: bfloat16 [768, 3072], P('dp', 'tensor'), may hold values from -0.21875 to 0.21875
- in_bias: bfloat16 [3072], P('dp'), may hold values from -3 to 3
- w_back: bfloat16 [3072, 768], P('tensor', 'dp'), may hold values from -0.15625 to 0.15625
- back_bias: bfloat16 [768], P('dp'), may hold values from -3 to 3
Outputs:
- output: bfloat16 [16384, 768], P(('dp', 'tensor'))
- grad_tokens: float32 [16384, 768], P(('dp', 'tensor'))
- grad_ln1_gain: float32 [768], P('dp')
- grad_ln1_bias: float32 [768], P('dp')
- grad_w_query: float32 [768, 768], P('dp', 'tensor')
- grad_query_bias: float32 [768], P('dp')
- grad_w_key: float32 [768, 768], P('dp', 'tensor')
- grad_w_value: float32 [768, 768], P('dp', 'tensor')
- grad_value_bias: float32 [768], P('dp')
- grad_w_out: float32 [768, 768], P('tensor', 'dp')
- grad_out_bias: float32 [768], P('dp')
- grad_ln2_gain: float32 [768], P('dp')
- grad_ln2_bias: float32 [768], P('dp')
- grad_w_in: float32 [768, 3072], P('dp', 'tensor')
- grad_in_bias: float32 [3072], P('dp')
- grad_w_back: float32 [3072, 768], P('tensor', 'dp')
- grad_back_bias: float32 [768], P('dp')
Inputs may be any that keep to these rules, and one draw needn't show every extreme that they name: `segment_ids`: in each sequence the document numbers never fall; every number 0 to 7 appears, on 1 to 512 consecutive patches, and some document has exactly 512.
All inputs are finite; a program needn't handle non-finite values.
Results may differ from a plain program's by a relative error of at most 0.02.
Values may be sent and summed in bfloat16 or wider, within the bound.
A program may use at most 128 MiB of HBM per device.

v0:
```python
import math
import jax
import jax.numpy as jnp
from jax import lax
from jax.sharding import PartitionSpec as P

HEAD_DIM = 64
EPSILON = 1e-12


def layer_norm(values, gain, shift):
    center = values - jnp.mean(values, axis=-1, keepdims=True)
    spread = jnp.mean(center * center, axis=-1, keepdims=True)
    return center * lax.rsqrt(spread + EPSILON) * gain + shift


def gelu_exact(values):
    return jax.nn.gelu(values, approximate=False)


def contract_rows(left, right):
    return lax.dot_general(
        left, right, (((0,), (0,)), ((), ())), preferred_element_type=jnp.float32
    )


def contract_cols(left, right):
    return lax.dot_general(
        left, right, (((1,), (1,)), ((), ())), preferred_element_type=jnp.float32
    )


def place_slice(length, piece, start):
    return lax.dynamic_update_slice_in_dim(jnp.zeros((length,), jnp.float32), piece, start, 0)


def per_device(
    tokens,
    cotangent,
    segment_ids,
    ln1_gain,
    ln1_bias,
    w_query,
    query_bias,
    w_key,
    w_value,
    value_bias,
    w_out,
    out_bias,
    ln2_gain,
    ln2_bias,
    w_in,
    in_bias,
    w_back,
    back_bias,
):
    f32 = jnp.float32
    bf16 = jnp.bfloat16
    index = lax.axis_index("tensor")
    (
        gain_one,
        shift_one,
        full_query,
        qbias_all,
        full_key,
        full_value,
        vbias_all,
        full_out,
        obias_all,
        gain_two,
        shift_two,
        full_in,
        ibias_all,
        full_back,
        bbias_all,
    ) = (
        lax.all_gather(ln1_gain, "dp", axis=0, tiled=True),
        lax.all_gather(ln1_bias, "dp", axis=0, tiled=True),
        lax.all_gather(w_query, "dp", axis=0, tiled=True),
        lax.all_gather(query_bias, "dp", axis=0, tiled=True),
        lax.all_gather(w_key, "dp", axis=0, tiled=True),
        lax.all_gather(w_value, "dp", axis=0, tiled=True),
        lax.all_gather(value_bias, "dp", axis=0, tiled=True),
        lax.all_gather(w_out, "dp", axis=1, tiled=True),
        lax.all_gather(out_bias, "dp", axis=0, tiled=True),
        lax.all_gather(ln2_gain, "dp", axis=0, tiled=True),
        lax.all_gather(ln2_bias, "dp", axis=0, tiled=True),
        lax.all_gather(w_in, "dp", axis=0, tiled=True),
        lax.all_gather(in_bias, "dp", axis=0, tiled=True),
        lax.all_gather(w_back, "dp", axis=1, tiled=True),
        lax.all_gather(back_bias, "dp", axis=0, tiled=True),
    )
    width = tokens.shape[1]
    head_width = full_query.shape[1]
    hidden_width = full_in.shape[1]
    unit_total = ibias_all.shape[0]
    local_heads = head_width // HEAD_DIM
    scale = HEAD_DIM ** (-0.5)
    gain_one = gain_one.astype(f32)
    shift_one = shift_one.astype(f32)
    gain_two = gain_two.astype(f32)
    shift_two = shift_two.astype(f32)
    query_shift = lax.dynamic_slice_in_dim(qbias_all, index * head_width, head_width).astype(f32)
    value_shift = lax.dynamic_slice_in_dim(vbias_all, index * head_width, head_width).astype(f32)
    unit_shift = lax.dynamic_slice_in_dim(ibias_all, index * hidden_width, hidden_width).astype(f32)
    inputs = tokens.astype(f32)
    act_one = layer_norm(inputs, gain_one, shift_one).astype(bf16)
    group_one = lax.all_gather(act_one, "tensor", axis=0, tiled=True)
    merged = jnp.concatenate([full_query, full_key, full_value], axis=1)
    mixed = jnp.dot(group_one, merged, preferred_element_type=f32)
    group = mixed.shape[0]
    seq_count = segment_ids.shape[0]
    seq_len = segment_ids.shape[1]
    query = (mixed[:, :head_width] + query_shift).astype(bf16).reshape(group, local_heads, HEAD_DIM)
    keys = (
        mixed[:, head_width : 2 * head_width]
        .astype(bf16)
        .reshape(seq_count, seq_len, local_heads, HEAD_DIM)
    )
    values = (
        (mixed[:, 2 * head_width :] + value_shift)
        .astype(bf16)
        .reshape(seq_count, seq_len, local_heads, HEAD_DIM)
    )
    block = math.gcd(512, seq_len)
    per_seq = seq_len // block
    block_count = group // block

    def block_scores(number):
        sequence = number // per_seq
        begin = number * block
        offset = begin - sequence * seq_len
        query_block = lax.dynamic_slice_in_dim(query, begin, block, 0)
        key_seq = lax.dynamic_index_in_dim(keys, sequence, 0, keepdims=False)
        value_seq = lax.dynamic_index_in_dim(values, sequence, 0, keepdims=False)
        doc_all = lax.dynamic_index_in_dim(segment_ids, sequence, 0, keepdims=False)
        doc_rows = lax.dynamic_slice_in_dim(doc_all, offset, block, 0)
        raw = jnp.einsum("qhd,khd->hqk", query_block, key_seq, preferred_element_type=f32)
        same = (doc_rows[:, None] == doc_all[None, :])[None]
        scores = jnp.where(same, raw * scale, -1000000000.0)
        return (scores, query_block, key_seq, value_seq, begin, sequence)

    def forward_block(number):
        scores, query_block, key_seq, value_seq, begin, sequence = block_scores(number)
        top = jnp.max(scores, axis=-1, keepdims=True)
        expo = jnp.exp(scores - top)
        denom = jnp.sum(expo, axis=-1, keepdims=True)
        weights = (expo / denom).astype(bf16)
        result = jnp.einsum("hqk,khd->qhd", weights, value_seq, preferred_element_type=f32)
        return (
            result.reshape(block, head_width).astype(bf16),
            top[..., 0] + jnp.log(denom[..., 0]),
        )

    context_blocks, lse_all = lax.map(forward_block, jnp.arange(block_count))
    context = context_blocks.reshape(group, head_width)
    attn_part = jnp.dot(context, full_out, preferred_element_type=f32).astype(bf16)
    attn_sum = lax.psum_scatter(attn_part, "tensor", scatter_dimension=0, tiled=True).astype(
        jnp.float32
    )
    middle = inputs + attn_sum + obias_all.astype(f32)
    act_two = layer_norm(middle, gain_two, shift_two).astype(bf16)
    group_two = lax.all_gather(act_two, "tensor", axis=0, tiled=True)
    pre = jnp.dot(group_two, full_in, preferred_element_type=f32) + unit_shift
    hidden = gelu_exact(pre).astype(bf16)
    mlp_part = jnp.dot(hidden, full_back, preferred_element_type=f32).astype(bf16)
    mlp_sum = lax.psum_scatter(mlp_part, "tensor", scatter_dimension=0, tiled=True).astype(
        jnp.float32
    )
    result = middle + mlp_sum + bbias_all.astype(f32)
    output = result.astype(bf16)
    back_query, back_key, back_value, back_out, back_in, back_back = (
        lax.all_gather(w_query, "dp", axis=0, tiled=True),
        lax.all_gather(w_key, "dp", axis=0, tiled=True),
        lax.all_gather(w_value, "dp", axis=0, tiled=True),
        lax.all_gather(w_out, "dp", axis=1, tiled=True),
        lax.all_gather(w_in, "dp", axis=0, tiled=True),
        lax.all_gather(w_back, "dp", axis=1, tiled=True),
    )
    merged_back = jnp.concatenate([back_query, back_key, back_value], axis=1)
    upstream = cotangent.astype(f32)
    back_bias_term = jnp.sum(upstream, axis=0)
    cot_rows = lax.all_gather(cotangent, "tensor", axis=0, tiled=True)
    grad_w_back = contract_rows(hidden, cot_rows)
    grad_hidden = contract_cols(cot_rows, back_back)
    gelu_out, gelu_pull = jax.vjp(gelu_exact, pre)
    grad_pre = gelu_pull(grad_hidden)[0]
    unit_term = jnp.sum(grad_pre, axis=0)
    pre_low = grad_pre.astype(bf16)
    grad_w_in = contract_rows(group_two, pre_low)
    grad_norm_two = lax.psum_scatter(
        contract_cols(pre_low, back_in).astype(jnp.bfloat16),
        "tensor",
        scatter_dimension=0,
        tiled=True,
    ).astype(jnp.float32)
    norm_out, norm_pull = jax.vjp(layer_norm, middle, gain_two, shift_two)
    grad_mid_norm, ln2_gain_term, ln2_bias_term = norm_pull(grad_norm_two)
    grad_middle = upstream + grad_mid_norm
    out_bias_term = jnp.sum(grad_middle, axis=0)
    middle_low = grad_middle.astype(bf16)
    middle_rows = lax.all_gather(middle_low, "tensor", axis=0, tiled=True)
    grad_w_out = contract_rows(context, middle_rows)
    grad_context = (
        contract_cols(middle_rows, back_out).astype(bf16).reshape(group, local_heads, HEAD_DIM)
    )

    def backward_block(carry, number):
        keys_acc, values_acc = carry
        scores, query_block, key_seq, value_seq, begin, sequence = block_scores(number)
        lse = lax.dynamic_index_in_dim(lse_all, number, 0, keepdims=False)
        probs = jnp.exp(scores - lse[:, :, None])
        weights = probs.astype(bf16)
        upstream_block = lax.dynamic_slice_in_dim(grad_context, begin, block, 0)
        grad_weights = jnp.einsum(
            "qhd,khd->hqk", upstream_block, value_seq, preferred_element_type=f32
        )
        delta = jnp.sum(grad_weights * probs, axis=-1, keepdims=True)
        grad_raw = (probs * (grad_weights - delta) * scale).astype(bf16)
        query_part = jnp.einsum("hqk,khd->qhd", grad_raw, key_seq, preferred_element_type=f32)
        key_part = jnp.einsum("hqk,qhd->khd", grad_raw, query_block, preferred_element_type=f32)
        value_part = jnp.einsum("hqk,qhd->khd", weights, upstream_block, preferred_element_type=f32)
        keys_acc = lax.dynamic_update_index_in_dim(
            keys_acc,
            lax.dynamic_index_in_dim(keys_acc, sequence, 0, keepdims=False) + key_part,
            sequence,
            0,
        )
        values_acc = lax.dynamic_update_index_in_dim(
            values_acc,
            lax.dynamic_index_in_dim(values_acc, sequence, 0, keepdims=False) + value_part,
            sequence,
            0,
        )
        return ((keys_acc, values_acc), query_part)

    empty = jnp.zeros((seq_count, seq_len, local_heads, HEAD_DIM), f32)
    (grad_keys, grad_values), query_parts = lax.scan(
        backward_block, (empty, empty), jnp.arange(block_count)
    )
    grad_query = query_parts.reshape(group, head_width)
    grad_keys = grad_keys.reshape(group, head_width)
    grad_values = grad_values.reshape(group, head_width)
    query_term = jnp.sum(grad_query, axis=0)
    value_term = jnp.sum(grad_values, axis=0)
    grad_lows = jnp.concatenate([grad_query, grad_keys, grad_values], axis=1).astype(bf16)
    grad_merged = contract_rows(group_one, grad_lows)
    grad_w_query = grad_merged[:, :head_width]
    grad_w_key = grad_merged[:, head_width : 2 * head_width]
    grad_w_value = grad_merged[:, 2 * head_width :]
    grad_norm_one = lax.psum_scatter(
        contract_cols(grad_lows, merged_back).astype(jnp.bfloat16),
        "tensor",
        scatter_dimension=0,
        tiled=True,
    ).astype(jnp.float32)
    first_out, first_pull = jax.vjp(layer_norm, inputs, gain_one, shift_one)
    grad_in_norm, ln1_gain_term, ln1_bias_term = first_pull(grad_norm_one)
    grad_tokens = grad_middle + grad_in_norm
    vectors = (
        lax.psum(ln1_gain_term.astype(jnp.bfloat16), "tensor").astype(jnp.float32),
        lax.psum(ln1_bias_term.astype(jnp.bfloat16), "tensor").astype(jnp.float32),
        lax.psum(
            place_slice(width, query_term, index * head_width).astype(jnp.bfloat16), "tensor"
        ).astype(jnp.float32),
        lax.psum(
            place_slice(width, value_term, index * head_width).astype(jnp.bfloat16), "tensor"
        ).astype(jnp.float32),
        lax.psum(out_bias_term.astype(jnp.bfloat16), "tensor").astype(jnp.float32),
        lax.psum(ln2_gain_term.astype(jnp.bfloat16), "tensor").astype(jnp.float32),
        lax.psum(ln2_bias_term.astype(jnp.bfloat16), "tensor").astype(jnp.float32),
        lax.psum(
            place_slice(unit_total, unit_term, index * hidden_width).astype(jnp.bfloat16), "tensor"
        ).astype(jnp.float32),
        lax.psum(back_bias_term.astype(jnp.bfloat16), "tensor").astype(jnp.float32),
    )
    (
        grad_w_query,
        grad_w_key,
        grad_w_value,
        grad_w_out,
        grad_w_in,
        grad_w_back,
        grad_ln1_gain,
        grad_ln1_bias,
        grad_query_bias,
        grad_value_bias,
        grad_out_bias,
        grad_ln2_gain,
        grad_ln2_bias,
        grad_in_bias,
        grad_back_bias,
    ) = (
        lax.psum_scatter(grad_w_query, "dp", scatter_dimension=0, tiled=True),
        lax.psum_scatter(grad_w_key, "dp", scatter_dimension=0, tiled=True),
        lax.psum_scatter(grad_w_value, "dp", scatter_dimension=0, tiled=True),
        lax.psum_scatter(grad_w_out, "dp", scatter_dimension=1, tiled=True),
        lax.psum_scatter(grad_w_in, "dp", scatter_dimension=0, tiled=True),
        lax.psum_scatter(grad_w_back, "dp", scatter_dimension=1, tiled=True),
        lax.psum_scatter(vectors[0], "dp", scatter_dimension=0, tiled=True),
        lax.psum_scatter(vectors[1], "dp", scatter_dimension=0, tiled=True),
        lax.psum_scatter(vectors[2], "dp", scatter_dimension=0, tiled=True),
        lax.psum_scatter(vectors[3], "dp", scatter_dimension=0, tiled=True),
        lax.psum_scatter(vectors[4], "dp", scatter_dimension=0, tiled=True),
        lax.psum_scatter(vectors[5], "dp", scatter_dimension=0, tiled=True),
        lax.psum_scatter(vectors[6], "dp", scatter_dimension=0, tiled=True),
        lax.psum_scatter(vectors[7], "dp", scatter_dimension=0, tiled=True),
        lax.psum_scatter(vectors[8], "dp", scatter_dimension=0, tiled=True),
    )
    return (
        output,
        grad_tokens,
        grad_ln1_gain,
        grad_ln1_bias,
        grad_w_query,
        grad_query_bias,
        grad_w_key,
        grad_w_value,
        grad_value_bias,
        grad_w_out,
        grad_out_bias,
        grad_ln2_gain,
        grad_ln2_bias,
        grad_w_in,
        grad_in_bias,
        grad_w_back,
        grad_back_bias,
    )


def solution(mesh):
    return jax.shard_map(
        per_device,
        mesh=mesh,
        in_specs=(
            P(("dp", "tensor"), None),
            P(("dp", "tensor"), None),
            P("dp", None),
            P("dp"),
            P("dp"),
            P("dp", "tensor"),
            P("dp"),
            P("dp", "tensor"),
            P("dp", "tensor"),
            P("dp"),
            P("tensor", "dp"),
            P("dp"),
            P("dp"),
            P("dp"),
            P("dp", "tensor"),
            P("dp"),
            P("tensor", "dp"),
            P("dp"),
        ),
        out_specs=(
            P(("dp", "tensor"), None),
            P(("dp", "tensor"), None),
            P("dp"),
            P("dp"),
            P("dp", "tensor"),
            P("dp"),
            P("dp", "tensor"),
            P("dp", "tensor"),
            P("dp"),
            P("tensor", "dp"),
            P("dp"),
            P("dp"),
            P("dp"),
            P("dp", "tensor"),
            P("dp"),
            P("tensor", "dp"),
            P("dp"),
        ),
        check_vma=False,
    )
```

profile of v0, /device:TPU:0, one launch (start us, length us, event | category | flops | bytes accessed | tf_op | source)
XLA Modules:
  0.0 1247.8 jit_solution(12022204815762069830)
XLA Ops:
  19.7 39.5 %all-reduce.18 = (bf16[768]{0:T(1024)(128)(2,1)S(1)}, bf16[768]{0:T(1024)(128)(2,1)S(1)}, bf16[768]{0:T(1024)(128)(2,1)S(1)}, bf16[768]{0:T(1024)(128)(2,1)S(1)}...) all-reduce(bf16[768]{0:T(1024)(128)(2,1)S(1)} %dynamic-update-slice, ...), channel_id=1, replica_groups=mesh['dp'=8,'tensor'=4] {'dp'}, use_global_device_ids=true, to_apply=%add.1 | all-reduce | flops 6144 | bytes 24576
  62.5 31.0 %all_gather.71 = bf16[192,768]{0,1:T(8,128)(2,1)S(1)} all-gather(bf16[192,96]{0,1:T(8,128)(2,1)S(1)} %copy.44), channel_id=1, replica_groups=mesh['dp'=8,'tensor'=4] {'dp'}, dimensions={1}, use_global_device_ids=true | all-gather | bytes 331776 | tf_op jit(solution)/shard_map/all_gather | solution.py:84
  93.5 31.0 %all_gather.66 = bf16[768,192]{1,0:T(8,128)(2,1)S(1)} all-gather(bf16[96,192]{1,0:T(8,128)(2,1)S(1)} %copy-done.36), channel_id=1, replica_groups=mesh['dp'=8,'tensor'=4] {'dp'}, dimensions={0}, use_global_device_ids=true | all-gather | bytes 331776 | tf_op jit(solution)/shard_map/all_gather | solution.py:79
  124.5 31.0 %all_gather.67 = bf16[768,192]{1,0:T(8,128)(2,1)S(1)} all-gather(bf16[96,192]{1,0:T(8,128)(2,1)S(1)} %copy-done.37), channel_id=1, replica_groups=mesh['dp'=8,'tensor'=4] {'dp'}, dimensions={0}, use_global_device_ids=true | all-gather | bytes 331776 | tf_op jit(solution)/shard_map/all_gather | solution.py:81
  155.5 31.1 %all_gather.68 = bf16[768,192]{1,0:T(8,128)(2,1)S(1)} all-gather(bf16[96,192]{1,0:T(8,128)(2,1)S(1)} %copy-done.38), channel_id=1, replica_groups=mesh['dp'=8,'tensor'=4] {'dp'}, dimensions={0}, use_global_device_ids=true | all-gather | bytes 331776 | tf_op jit(solution)/shard_map/all_gather | solution.py:82
  191.6 98.7 %while.30 = (s32[]{:T(128)}, bf16[4,512,192]{1,2,0:T(8,128)(2,1)}, f32[4,3,512]{2,1,0:T(4,128)S(1)}, s32[4]{0:T(128)S(1)}, s32[1,2048]{1,0:T(1,128)S(1)}, /*inde...) while((s32[]{:T(128)}, bf16[4,512,192]{1,2,0:T(8,128)(2,1)}, ...), condition=%wide.region_5.6_spmd, body=%wide.region_2.5_spmd.sunk | while | flops 844200448 | bytes 44372400 | solution.py:155
  296.1 34.7 %reduce-scatter.19.cloned.1.call-done = bf16[512,768]{1,0:T(8,128)(2,1)} async-done(((bf16[2048,768]{1,0:T(8,128)(2,1)}), bf16[512,768]{1,0:T(8,128)(2,1)}) %reduce-scatter.19.cloned.1.call-update) | async-done | bytes 786448 | tf_op jit(solution)/shard_map/reduce_scatter | solution.py:158
  336.7 26.4 %all-gather = bf16[8,1,384]{2,1,0:T(2,128)(2,1)S(1)} all-gather(bf16[1,1,384]{2,1,0:T(2,128)(2,1)S(1)} %reshape.282), channel_id=1, replica_groups=mesh['dp'=8,'tensor'=4] {'dp'}, dimensions={0}, use_global_device_ids=true | all-gather | bytes 6912 | tf_op jit(solution)/shard_map/all_gather | solution.py:89
  373.6 36.3 %all-gather.14.cloned.1.call-done = bf16[768,768]{0,1:T(8,128)(2,1)} async-done(((bf16[768,96]{0,1:T(8,128)(2,1)}), bf16[768,768]{0,1:T(8,128)(2,1)}) %all-gather.14.cloned.1.call-update) | async-done | bytes 1179664 | tf_op jit(solution)/shard_map/all_gather | solution.py:90
  409.9 28.5 %all-gather.16.cloned.1.call-done = bf16[2048,768]{1,0:T(8,128)(2,1)} async-done(((bf16[512,768]{1,0:T(8,128)(2,1)}), bf16[2048,768]{1,0:T(8,128)(2,1)}) %all-gather.16.cloned.1.call-update) | async-done | bytes 3145744 | tf_op jit(solution)/shard_map/all_gather | solution.py:183
  476.8 26.1 %reduce-scatter.23.cloned.1.call-done = bf16[512,768]{1,0:T(8,128)(2,1)} async-done(((bf16[2048,768]{1,0:T(8,128)(2,1)}), bf16[512,768]{1,0:T(8,128)(2,1)}) %reduce-scatter.23.cloned.1.call-update) | async-done | bytes 786448 | tf_op jit(solution)/shard_map/reduce_scatter | solution.py:191
  507.4 35.9 %reduce-scatter.21.cloned.1.call-done = bf16[512,768]{1,0:T(8,128)(2,1)} async-done(((bf16[2048,768]{1,0:T(8,128)(2,1)}), bf16[512,768]{1,0:T(8,128)(2,1)}) %reduce-scatter.21.cloned.1.call-update) | async-done | bytes 786448 | tf_op jit(solution)/shard_map/reduce_scatter | solution.py:167
  549.5 28.4 %all-gather.18.cloned.1.call-done = bf16[2048,768]{1,0:T(8,128)(2,1)} async-done(((bf16[512,768]{1,0:T(8,128)(2,1)}), bf16[2048,768]{1,0:T(8,128)(2,1)}) %all-gather.18.cloned.1.call-update) | async-done | bytes 3145744 | tf_op jit(solution)/shard_map/all_gather | solution.py:202
  588.9 258.0 %while.31 = (s32[]{:T(128)}, f32[1,2048,3,64]{1,3,2,0:T(8,128)}, f32[1,2048,3,64]{1,3,2,0:T(8,128)}, f32[4,512,3,64]{1,3,2,0:T(8,128)}, s32[4]{0:T(128)S(1)}, /*...) while((s32[]{:T(128)}, f32[1,2048,3,64]{1,3,2,0:T(8,128)}, ...), condition=%wide.region_15.16_spmd, body=%wide.region_13.15_spmd.sunk | while | flops 2096897024 | bytes 208079408 | solution.py:238
  610.3 20.9 %fusion.194 = f32[4,512,3,64]{1,3,2,0:T(8,128)} fusion(f32[4,512,3,64]{1,3,2,0:T(8,128)} %get-tuple-element.595, s32[]{:T(128)S(6)} %copy.83, f32[3,512,2048]{2,1,0:T(8,128)} %fusion.190, f32[3,512,2048]{2,1,0:T(8,128)} %copy-done, f32[3,512]{1,0:T(4,128)S(1)} %dynamic-slice_bitcast_fusion.2, pred[512,2048]{1,0:T(8,128)(4,1)S(1)} %broadcast_compare_fusion.5, ...), kind=kOutput, calls=%fused_computation.44.clone.1 | convolution fusion | flops 437259776 | bytes 53624836 | tf_op jit(solution)/shard_map/while/body/eval_jaxpr/hqk,khd->qhd/dot_general | solution.py:220
  631.2 22.6 %fusion.192 = f32[1,2048,3,64]{1,3,2,0:T(8,128)} fusion(f32[3,512,2048]{2,1,0:T(8,128)} %fusion.190, f32[3,512,2048]{2,1,0:T(8,128)} %copy-done, f32[3,512]{1,0:T(4,128)S(1)} %dynamic-slice_bitcast_fusion.2, pred[512,2048]{1,0:T(8,128)(4,1)S(1)} %broadcast_compare_fusion.5, f32[1,2048,3,64]{1,3,2,0:T(8,128)} %get-tuple-element.593, ...), kind=kOutput, calls=%fused_computation.39.clone.1 | convolution fusion | flops 437652992 | bytes 55787524 | tf_op jit(solution)/shard_map/while/body/eval_jaxpr/hqk,qhd->khd/dot_general | solution.py:221
  695.7 22.4 %fusion.192 = f32[1,2048,3,64]{1,3,2,0:T(8,128)} fusion(f32[3,512,2048]{2,1,0:T(8,128)} %fusion.190, f32[3,512,2048]{2,1,0:T(8,128)} %copy-done, f32[3,512]{1,0:T(4,128)S(1)} %dynamic-slice_bitcast_fusion.2, pred[512,2048]{1,0:T(8,128)(4,1)S(1)} %broadcast_compare_fusion.5, f32[1,2048,3,64]{1,3,2,0:T(8,128)} %get-tuple-element.593, ...), kind=kOutput, calls=%fused_computation.39.clone.1 | convolution fusion | flops 437652992 | bytes 55787524 | tf_op jit(solution)/shard_map/while/body/eval_jaxpr/hqk,qhd->khd/dot_general | solution.py:221
  760.0 22.4 %fusion.192 = f32[1,2048,3,64]{1,3,2,0:T(8,128)} fusion(f32[3,512,2048]{2,1,0:T(8,128)} %fusion.190, f32[3,512,2048]{2,1,0:T(8,128)} %copy-done, f32[3,512]{1,0:T(4,128)S(1)} %dynamic-slice_bitcast_fusion.2, pred[512,2048]{1,0:T(8,128)(4,1)S(1)} %broadcast_compare_fusion.5, f32[1,2048,3,64]{1,3,2,0:T(8,128)} %get-tuple-element.593, ...), kind=kOutput, calls=%fused_computation.39.clone.1 | convolution fusion | flops 437652992 | bytes 55787524 | tf_op jit(solution)/shard_map/while/body/eval_jaxpr/hqk,qhd->khd/dot_general | solution.py:221
  824.3 22.4 %fusion.192 = f32[1,2048,3,64]{1,3,2,0:T(8,128)} fusion(f32[3,512,2048]{2,1,0:T(8,128)} %fusion.190, f32[3,512,2048]{2,1,0:T(8,128)} %copy-done, f32[3,512]{1,0:T(4,128)S(1)} %dynamic-slice_bitcast_fusion.2, pred[512,2048]{1,0:T(8,128)(4,1)S(1)} %broadcast_compare_fusion.5, f32[1,2048,3,64]{1,3,2,0:T(8,128)} %get-tuple-element.593, ...), kind=kOutput, calls=%fused_computation.39.clone.1 | convolution fusion | flops 437652992 | bytes 55787524 | tf_op jit(solution)/shard_map/while/body/eval_jaxpr/hqk,qhd->khd/dot_general | solution.py:221
  912.1 38.8 %all-reduce.17 = (f32[768]{0:T(1024)S(1)}, f32[768]{0:T(1024)S(1)}, f32[768]{0:T(1024)S(1)}, f32[768]{0:T(1024)S(1)}, f32[768]{0:T(1024)S(1)}, /*index=5*/f32[76...) all-reduce(bf16[768]{0:T(1024)(128)(2,1)S(1)} %get-tuple-element.37, ...), channel_id=6, replica_groups=mesh['dp'=8,'tensor'=4] {'dp'}, use_global_device_ids=true, to_apply=%region_21.22.clone | all-reduce | flops 9216 | bytes 55296
  970.7 72.6 %reduce-scatter.27.cloned.1.call-done = f32[96,768]{1,0:T(8,128)} async-done(((f32[768,768]{1,0:T(8,128)}), f32[96,768]{1,0:T(8,128)}) %reduce-scatter.27.cloned.1.call-update) | async-done | bytes 294928 | tf_op jit(solution)/shard_map/reduce_scatter | solution.py:298
  1043.2 65.9 %reduce-scatter.35.cloned.1.call-done = f32[96,192]{1,0:T(8,128)} async-done(((f32[768,192]{1,0:T(8,128)}), f32[96,192]{1,0:T(8,128)}) %reduce-scatter.35.cloned.1.call-update) | async-done | bytes 73744
  1109.2 65.4 %reduce-scatter.33.cloned.1.call-done = f32[96,192]{1,0:T(8,128)} async-done(((f32[768,192]{1,0:T(8,128)}), f32[96,192]{1,0:T(8,128)}) %reduce-scatter.33.cloned.1.call-update) | async-done | bytes 73744
  1174.5 65.9 %reduce-scatter.31.cloned.1.call-done = f32[96,192]{1,0:T(8,128)} async-done(((f32[768,192]{1,0:T(8,128)}), f32[96,192]{1,0:T(8,128)}) %reduce-scatter.31.cloned.1.call-update) | async-done | bytes 73744
  (321 shorter events, 398.4 us)
Async XLA Ops:
  8.0 54.3 %copy-start.39 = (bf16[192,96]{1,0:T(8,128)(2,1)S(1)}, bf16[192,96]{1,0:T(8,128)(2,1)}, u32[]{:S(2)}) copy-start(bf16[192,96]{1,0:T(8,128)(2,1)} %param.32) | copy-start | bytes 110596
  8.0 85.5 %copy-start.36 = (bf16[96,192]{1,0:T(8,128)(2,1)S(1)}, bf16[96,192]{1,0:T(8,128)(2,1)}, u32[]{:S(2)}) copy-start(bf16[96,192]{1,0:T(8,128)(2,1)} %param.27) | copy-start | bytes 110596
  8.0 116.4 %copy-start.37 = (bf16[96,192]{1,0:T(8,128)(2,1)S(1)}, bf16[96,192]{1,0:T(8,128)(2,1)}, u32[]{:S(2)}) copy-start(bf16[96,192]{1,0:T(8,128)(2,1)} %param.29) | copy-start | bytes 110596
  8.1 147.4 %copy-start.38 = (bf16[96,192]{1,0:T(8,128)(2,1)S(1)}, bf16[96,192]{1,0:T(8,128)(2,1)}, u32[]{:S(2)}) copy-start(bf16[96,192]{1,0:T(8,128)(2,1)} %param.30) | copy-start | bytes 110596
  8.1 178.5 %all-gather.8.cloned.1.call-start = ((), (), s32[]{:S(2)}) async-start(), calls=%async_computation.10 | async-start | bytes 3932160 | tf_op jit(solution)/shard_map/all_gather | solution.py:108
  62.2 268.6 %reduce-scatter.19.cloned.1.call-start = ((), (), s32[]{:S(2)}) async-start(), calls=%async_computation.11 | async-start | bytes 3932160 | tf_op jit(solution)/shard_map/reduce_scatter | solution.py:158
  93.5 198.3 %copy-start.13 = (bf16[192,768]{0,1:T(8,128)(2,1)}, bf16[192,768]{0,1:T(8,128)(2,1)S(1)}, u32[]{:S(2)}) copy-start(bf16[192,768]{0,1:T(8,128)(2,1)S(1)} %all_gather.71) | copy-start | bytes 884740
  124.5 62.1 %copy-start.26 = (bf16[768,192]{1,0:T(8,128)(2,1)}, bf16[768,192]{1,0:T(8,128)(2,1)S(1)}, u32[]{:S(2)}) copy-start(bf16[768,192]{1,0:T(8,128)(2,1)S(1)} %all_gather.66) | copy-start | bytes 884740
  295.4 67.8 %all-gather.12.cloned.1.call-start = ((), (), s32[]{:S(2)}) async-start(), calls=%async_computation.13 | async-start | bytes 1327104 | tf_op jit(solution)/shard_map/all_gather | solution.py:88
  296.0 70.1 %all-gather.10.cloned.1.call-start = ((), (), s32[]{:S(2)}) async-start(), calls=%async_computation.12 | async-start | bytes 3932160 | tf_op jit(solution)/shard_map/all_gather | solution.py:163
  335.3 74.6 %all-gather.14.cloned.1.call-start = ((), (), s32[]{:S(2)}) async-start(), calls=%async_computation.14 | async-start | bytes 1327104 | tf_op jit(solution)/shard_map/all_gather | solution.py:90
  335.9 102.6 %all-gather.16.cloned.1.call-start = ((), (), s32[]{:S(2)}) async-start(), calls=%async_computation.16 | async-start | bytes 3932160 | tf_op jit(solution)/shard_map/all_gather | solution.py:183
  336.7 166.2 %reduce-scatter.23.cloned.1.call-start = ((), (), s32[]{:S(2)}) async-start(), calls=%async_computation.17 | async-start | bytes 3932160 | tf_op jit(solution)/shard_map/reduce_scatter | solution.py:191
  464.8 78.5 %reduce-scatter.21.cloned.1.call-start = ((), (), s32[]{:S(2)}) async-start(), calls=%async_computation.15 | async-start | bytes 3932160 | tf_op jit(solution)/shard_map/reduce_scatter | solution.py:167
  476.1 101.8 %all-gather.18.cloned.1.call-start = ((), (), s32[]{:S(2)}) async-start(), calls=%async_computation.18 | async-start | bytes 3932160 | tf_op jit(solution)/shard_map/all_gather | solution.py:202
  549.4 336.2 %reduce-scatter.37.cloned.1.call-start = ((), (), s32[]{:S(2)}) async-start(), calls=%async_computation.25 | async-start | bytes 884736
  582.1 314.7 %reduce-scatter.25.cloned.1.call-start = ((), (), s32[]{:S(2)}) async-start(), calls=%async_computation.19 | async-start | bytes 3932160 | tf_op jit(solution)/shard_map/reduce_scatter | solution.py:251
  858.8 111.9 %reduce-scatter.29.cloned.1.call-start = ((), (), s32[]{:S(2)}) async-start(), calls=%async_computation.21 | async-start | bytes 2654208 | tf_op jit(solution)/shard_map/reduce_scatter | solution.py:299
  866.7 176.5 %reduce-scatter.27.cloned.1.call-start = ((), (), s32[]{:S(2)}) async-start(), calls=%async_computation.20 | async-start | bytes 2654208 | tf_op jit(solution)/shard_map/reduce_scatter | solution.py:298
  874.3 234.8 %reduce-scatter.35.cloned.1.call-start = ((), (), s32[]{:S(2)}) async-start(), calls=%async_computation.24 | async-start | bytes 884736
  879.6 294.9 %reduce-scatter.33.cloned.1.call-start = ((), (), s32[]{:S(2)}) async-start(), calls=%async_computation.23 | async-start | bytes 884736
  880.9 359.5 %reduce-scatter.31.cloned.1.call-start = ((), (), s32[]{:S(2)}) async-start(), calls=%async_computation.22 | async-start | bytes 884736
  884.0 72.3 %copy-start.5 = (f32[512,768]{1,0:T(8,128)S(1)}, f32[512,768]{1,0:T(8,128)}, u32[]{:S(2)}) copy-start(f32[512,768]{1,0:T(8,128)} %copy-done.4) | copy-start | bytes 4718596
  896.7 59.5 %copy-start.7 = (bf16[512,768]{1,0:T(8,128)(2,1)S(1)}, bf16[512,768]{1,0:T(8,128)(2,1)}, u32[]{:S(2)}) copy-start(bf16[512,768]{1,0:T(8,128)(2,1)} %reduce-scatter.25.cloned.1.call-done) | copy-start | bytes 2359300
  (50 other events, 568.3 us)
Sparse Core Ops, SparseCore 0:
  62.3 25.7 all-gather.7
  295.5 35.2 reduce-scatter.18
  464.9 37.9 reduce-scatter.22
  505.2 37.9 reduce-scatter.20
Sparse Core Ops, SparseCore 1:
  298.3 38.8 all-gather.11
  339.2 26.8 all-gather.9
  368.4 41.5 all-gather.13
  411.6 26.8 all-gather.15
  549.5 28.3 all-gather.17
  582.1 62.5 reduce-scatter.36
  858.9 37.8 reduce-scatter.24
  901.1 69.5 reduce-scatter.28
  975.0 68.2 reduce-scatter.26
  1047.5 61.6 reduce-scatter.34
  1112.9 61.6 reduce-scatter.32
  1178.8 61.6 reduce-scatter.30
where the time goes:
time: 1250 us
  waiting for transfers between devices  487 us (39%)
  matrix products  358 us (29%)
  blocking collectives  239 us (19%)
  other arithmetic  70.1 us (6%)
  local copies, waits for them, and re-layouts  42.9 us (3%)
  loops' own time  31.9 us (3%)
  between operations  18.4 us (1%)
    unnamed x20, waiting for transfers between devices  199 us
    dot_general x4, matrix products, backward_block(): jnp.einsum('hqk,qhd->khd', grad_raw, query_block, preferred_element_type=...  89.7 us
    dot_general x4, matrix products, backward_block(): jnp.einsum('hqk,khd->qhd', grad_raw, key_seq, preferred_element_type=f32)  83.1 us
    unnamed x2, blocking collectives  78.3 us
    reduce_scatter x1, waiting for transfers between devices, per_device(): lax.psum_scatter(grad_w_in, 'dp', scatter_dimension=0, tiled=True)  72.6 us
    all_gather x1, waiting for transfers between devices, per_device(): lax.all_gather(w_back, 'dp', axis=1, tiled=True)  36.3 us
    reduce_scatter x1, waiting for transfers between devices, per_device(): lax.psum_scatter(mlp_part, 'tensor', scatter_dimension=0, tiled=True)  35.9 us
    reduce_scatter x1, waiting for transfers between devices, per_device(): lax.psum_scatter(attn_part, 'tensor', scatter_dimension=0, tiled=True)  34.7 us
  transfers between devices with their start and end apart: 16, of which 13 were waited for; matrix products, arithmetic and copies ran while one was open for 26% of the time, Pallas kernels for 0%

commit v1 on v0

--- a/solution.py
+++ b/solution.py
@@ -180,7 +180,28 @@
     merged_back = jnp.concatenate([back_query, back_key, back_value], axis=1)
     upstream = cotangent.astype(f32)
     back_bias_term = jnp.sum(upstream, axis=0)
-    cot_rows = lax.all_gather(cotangent, "tensor", axis=0, tiled=True)
+
+    def play_edge(state, net_axis):
+        piece_next = lax.axis_index(net_axis)
+        field_out = lax.axis_size(net_axis)
+        near, t1, finding = (field_out, piece_next, state.shape[0])
+        grid = tuple((p * near if u == 0 else p for u, p in enumerate(state.shape)))
+        plain = jnp.zeros(grid, state.dtype)
+        moved = r2 = state
+        b_now = lax.dynamic_update_slice_in_dim(plain, state, t1 * finding, axis=0)
+        for idx in range(1, near // 2 + 1):
+            moved = lax.ppermute(moved, net_axis, tuple(((u, (u + 1) % near) for u in range(near))))
+            b_now = lax.dynamic_update_slice_in_dim(
+                b_now, moved, (t1 - idx) % near * finding, axis=0
+            )
+            if 2 * idx < near:
+                r2 = lax.ppermute(r2, net_axis, tuple(((u, (u - 1) % near) for u in range(near))))
+                b_now = lax.dynamic_update_slice_in_dim(
+                    b_now, r2, (t1 + idx) % near * finding, axis=0
+                )
+        return b_now
+
+    cot_rows = play_edge(cotangent, "tensor")
     grad_w_back = contract_rows(hidden, cot_rows)
     grad_hidden = contract_cols(cot_rows, back_back)
     gelu_out, gelu_pull = jax.vjp(gelu_exact, pre)

time: 1250 us -> 1230 us (0.984)
  waiting for transfers between devices: 487 us -> 457 us
    all_gather x1 -> x0, waiting for transfers between devices: 28.5 us -> none  [per_device(): cot_rows = lax.all_gather(cotangent, 'tensor', axis=0, tiled=True)]
    ppermute x0 -> x3, waiting for transfers between devices: none -> 24.9 us  [the longest x2 24.9 us: play_edge(): lax.ppermute(moved, net_axis, tuple(((u, (u + 1) % near) for u in range(n...]
    all_gather x1, waiting for transfers between devices: 36.3 us -> 16.2 us  [per_device(): lax.all_gather(w_back, 'dp', axis=1, tiled=True)]
    unnamed x134 -> x122, local copies, waits for them, and re-layouts: 28.6 us -> 27.2 us
    unnamed x20 -> x19, waiting for transfers between devices: 199 us -> 198 us
  transfers between devices with their start and end apart: 16 -> 18, of which waited for: 13 -> 12; matrix products, arithmetic and copies ran while one was open for 26% -> 27% of each run, Pallas kernels for 0% -> 0%
where the time goes in v1:
time: 1230 us
  waiting for transfers between devices  457 us (37%)
  matrix products  359 us (29%)
  blocking collectives  238 us (19%)
  other arithmetic  71 us (6%)
  local copies, waits for them, and re-layouts  49.7 us (4%)
  loops' own time  31.9 us (3%)
  between operations  18.3 us (1%)
    unnamed x19, waiting for transfers between devices  198 us
    dot_general x4, matrix products, backward_block(): jnp.einsum('hqk,qhd->khd', grad_raw, query_block, preferred_element_type=...  89.9 us
    dot_general x4, matrix products, backward_block(): jnp.einsum('hqk,khd->qhd', grad_raw, key_seq, preferred_element_type=f32)  83.1 us
    unnamed x2, blocking collectives  77.7 us
    reduce_scatter x1, waiting for transfers between devices, per_device(): lax.psum_scatter(grad_w_in, 'dp', scatter_dimension=0, tiled=True)  72.5 us
    reduce_scatter x1, waiting for transfers between devices, per_device(): lax.psum_scatter(mlp_part, 'tensor', scatter_dimension=0, tiled=True)  35.9 us
    reduce_scatter x1, waiting for transfers between devices, per_device(): lax.psum_scatter(attn_part, 'tensor', scatter_dimension=0, tiled=True)  34.8 us
    dot_general x4, matrix products, contract_cols(): lax.dot_general(left, right, (((1,), (1,)), ((), ())), preferred_element_...  33.2 us
  transfers between devices with their start and end apart: 18, of which 12 were waited for; matrix products, arithmetic and copies ran while one was open for 27% of the time, Pallas kernels for 0%

profile of v1, /device:TPU:0, one launch (start us, length us, event | category | flops | bytes accessed | tf_op | source)
XLA Modules:
  0.0 1228.0 jit_solution(13960310975743180764)
XLA Ops:
  19.7 39.4 %all-reduce.18 = (bf16[768]{0:T(1024)(128)(2,1)S(1)}, bf16[768]{0:T(1024)(128)(2,1)S(1)}, bf16[768]{0:T(1024)(128)(2,1)S(1)}, bf16[768]{0:T(1024)(128)(2,1)S(1)}...) all-reduce(bf16[768]{0:T(1024)(128)(2,1)S(1)} %dynamic-update-slice, ...), channel_id=1, replica_groups=mesh['dp'=8,'tensor'=4] {'dp'}, use_global_device_ids=true, to_apply=%add.1 | all-reduce | flops 6144 | bytes 24576
  61.8 31.0 %all_gather.68 = bf16[192,768]{0,1:T(8,128)(2,1)S(1)} all-gather(bf16[192,96]{0,1:T(8,128)(2,1)S(1)} %copy.44), channel_id=1, replica_groups=mesh['dp'=8,'tensor'=4] {'dp'}, dimensions={1}, use_global_device_ids=true | all-gather | bytes 331776 | tf_op jit(solution)/shard_map/all_gather | solution.py:84
  92.8 31.0 %all_gather.63 = bf16[768,192]{1,0:T(8,128)(2,1)S(1)} all-gather(bf16[96,192]{1,0:T(8,128)(2,1)S(1)} %copy-done.29), channel_id=1, replica_groups=mesh['dp'=8,'tensor'=4] {'dp'}, dimensions={0}, use_global_device_ids=true | all-gather | bytes 331776 | tf_op jit(solution)/shard_map/all_gather | solution.py:79
  123.8 31.0 %all_gather.64 = bf16[768,192]{1,0:T(8,128)(2,1)S(1)} all-gather(bf16[96,192]{1,0:T(8,128)(2,1)S(1)} %copy-done.30), channel_id=1, replica_groups=mesh['dp'=8,'tensor'=4] {'dp'}, dimensions={0}, use_global_device_ids=true | all-gather | bytes 331776 | tf_op jit(solution)/shard_map/all_gather | solution.py:81
  154.8 31.1 %all_gather.65 = bf16[768,192]{1,0:T(8,128)(2,1)S(1)} all-gather(bf16[96,192]{1,0:T(8,128)(2,1)S(1)} %copy-done.31), channel_id=1, replica_groups=mesh['dp'=8,'tensor'=4] {'dp'}, dimensions={0}, use_global_device_ids=true | all-gather | bytes 331776 | tf_op jit(solution)/shard_map/all_gather | solution.py:82
  191.5 98.6 %while.30 = (s32[]{:T(128)}, bf16[4,512,192]{1,2,0:T(8,128)(2,1)}, f32[4,3,512]{2,1,0:T(4,128)S(1)}, s32[4]{0:T(128)S(1)}, s32[1,2048]{1,0:T(1,128)S(1)}, /*inde...) while((s32[]{:T(128)}, bf16[4,512,192]{1,2,0:T(8,128)(2,1)}, ...), condition=%wide.region_5.6_spmd, body=%wide.region_2.5_spmd.sunk | while | flops 844200448 | bytes 44372400 | solution.py:155
  295.9 34.8 %reduce-scatter.19.cloned.1.call-done = bf16[512,768]{1,0:T(8,128)(2,1)} async-done(((bf16[2048,768]{1,0:T(8,128)(2,1)}), bf16[512,768]{1,0:T(8,128)(2,1)}) %reduce-scatter.19.cloned.1.call-update) | async-done | bytes 786448 | tf_op jit(solution)/shard_map/reduce_scatter | solution.py:158
  337.2 24.9 %collective-permute-done = bf16[512,768]{1,0:T(8,128)(2,1)} collective-permute-done((bf16[512,768]{1,0:T(8,128)(2,1)}, bf16[512,768]{1,0:T(8,128)(2,1)}, u32[]{:S(2)}, u32[]{:S(2)}) %collective-permute-start) | collective-permute-done | bytes 786464 | tf_op jit(solution)/shard_map/ppermute | solution.py:193
  362.0 26.3 %all-gather = bf16[8,1,384]{2,1,0:T(2,128)(2,1)S(1)} all-gather(bf16[1,1,384]{2,1,0:T(2,128)(2,1)S(1)} %reshape.282), channel_id=1, replica_groups=mesh['dp'=8,'tensor'=4] {'dp'}, dimensions={0}, use_global_device_ids=true | all-gather | bytes 6912 | tf_op jit(solution)/shard_map/all_gather | solution.py:89
  460.8 23.8 %reduce-scatter.23.cloned.1.call-done = bf16[512,768]{1,0:T(8,128)(2,1)} async-done(((bf16[2048,768]{1,0:T(8,128)(2,1)}), bf16[512,768]{1,0:T(8,128)(2,1)}) %reduce-scatter.23.cloned.1.call-update) | async-done | bytes 786448 | tf_op jit(solution)/shard_map/reduce_scatter | solution.py:212
  489.1 35.9 %reduce-scatter.21.cloned.1.call-done = bf16[512,768]{1,0:T(8,128)(2,1)} async-done(((bf16[2048,768]{1,0:T(8,128)(2,1)}), bf16[512,768]{1,0:T(8,128)(2,1)}) %reduce-scatter.21.cloned.1.call-update) | async-done | bytes 786448 | tf_op jit(solution)/shard_map/reduce_scatter | solution.py:167
  531.2 28.6 %all-gather.15.cloned.1.call-done = bf16[2048,768]{1,0:T(8,128)(2,1)} async-done(((bf16[512,768]{1,0:T(8,128)(2,1)}), bf16[2048,768]{1,0:T(8,128)(2,1)}) %all-gather.15.cloned.1.call-update) | async-done | bytes 3145744 | tf_op jit(solution)/shard_map/all_gather | solution.py:223
  570.8 258.2 %while.31 = (s32[]{:T(128)}, f32[1,2048,3,64]{1,3,2,0:T(8,128)}, f32[1,2048,3,64]{1,3,2,0:T(8,128)}, f32[4,512,3,64]{1,3,2,0:T(8,128)}, s32[4]{0:T(128)S(1)}, /*...) while((s32[]{:T(128)}, f32[1,2048,3,64]{1,3,2,0:T(8,128)}, ...), condition=%wide.region_15.16_spmd, body=%wide.region_13.15_spmd.sunk | while | flops 2096897024 | bytes 208079408 | solution.py:259
  592.2 20.9 %fusion.195 = f32[4,512,3,64]{1,3,2,0:T(8,128)} fusion(f32[4,512,3,64]{1,3,2,0:T(8,128)} %get-tuple-element.597, s32[]{:T(128)S(6)} %copy.87, f32[3,512,2048]{2,1,0:T(8,128)} %fusion.191, f32[3,512,2048]{2,1,0:T(8,128)} %copy-done, f32[3,512]{1,0:T(4,128)S(1)} %dynamic-slice_bitcast_fusion.2, pred[512,2048]{1,0:T(8,128)(4,1)S(1)} %broadcast_compare_fusion.5, ...), kind=kOutput, calls=%fused_computation.44.clone.1 | convolution fusion | flops 437259776 | bytes 53624836 | tf_op jit(solution)/shard_map/while/body/eval_jaxpr/hqk,khd->qhd/dot_general | solution.py:241
  613.1 22.6 %fusion.193 = f32[1,2048,3,64]{1,3,2,0:T(8,128)} fusion(f32[3,512,2048]{2,1,0:T(8,128)} %fusion.191, f32[3,512,2048]{2,1,0:T(8,128)} %copy-done, f32[3,512]{1,0:T(4,128)S(1)} %dynamic-slice_bitcast_fusion.2, pred[512,2048]{1,0:T(8,128)(4,1)S(1)} %broadcast_compare_fusion.5, f32[1,2048,3,64]{1,3,2,0:T(8,128)} %get-tuple-element.595, ...), kind=kOutput, calls=%fused_computation.39.clone.1 | convolution fusion | flops 437652992 | bytes 55787524 | tf_op jit(solution)/shard_map/while/body/eval_jaxpr/hqk,qhd->khd/dot_general | solution.py:242
  677.6 22.5 %fusion.193 = f32[1,2048,3,64]{1,3,2,0:T(8,128)} fusion(f32[3,512,2048]{2,1,0:T(8,128)} %fusion.191, f32[3,512,2048]{2,1,0:T(8,128)} %copy-done, f32[3,512]{1,0:T(4,128)S(1)} %dynamic-slice_bitcast_fusion.2, pred[512,2048]{1,0:T(8,128)(4,1)S(1)} %broadcast_compare_fusion.5, f32[1,2048,3,64]{1,3,2,0:T(8,128)} %get-tuple-element.595, ...), kind=kOutput, calls=%fused_computation.39.clone.1 | convolution fusion | flops 437652992 | bytes 55787524 | tf_op jit(solution)/shard_map/while/body/eval_jaxpr/hqk,qhd->khd/dot_general | solution.py:242
  741.9 22.5 %fusion.193 = f32[1,2048,3,64]{1,3,2,0:T(8,128)} fusion(f32[3,512,2048]{2,1,0:T(8,128)} %fusion.191, f32[3,512,2048]{2,1,0:T(8,128)} %copy-done, f32[3,512]{1,0:T(4,128)S(1)} %dynamic-slice_bitcast_fusion.2, pred[512,2048]{1,0:T(8,128)(4,1)S(1)} %broadcast_compare_fusion.5, f32[1,2048,3,64]{1,3,2,0:T(8,128)} %get-tuple-element.595, ...), kind=kOutput, calls=%fused_computation.39.clone.1 | convolution fusion | flops 437652992 | bytes 55787524 | tf_op jit(solution)/shard_map/while/body/eval_jaxpr/hqk,qhd->khd/dot_general | solution.py:242
  785.6 20.8 %fusion.195 = f32[4,512,3,64]{1,3,2,0:T(8,128)} fusion(f32[4,512,3,64]{1,3,2,0:T(8,128)} %get-tuple-element.597, s32[]{:T(128)S(6)} %copy.87, f32[3,512,2048]{2,1,0:T(8,128)} %fusion.191, f32[3,512,2048]{2,1,0:T(8,128)} %copy-done, f32[3,512]{1,0:T(4,128)S(1)} %dynamic-slice_bitcast_fusion.2, pred[512,2048]{1,0:T(8,128)(4,1)S(1)} %broadcast_compare_fusion.5, ...), kind=kOutput, calls=%fused_computation.44.clone.1 | convolution fusion | flops 437259776 | bytes 53624836 | tf_op jit(solution)/shard_map/while/body/eval_jaxpr/hqk,khd->qhd/dot_general | solution.py:241
  806.4 22.5 %fusion.193 = f32[1,2048,3,64]{1,3,2,0:T(8,128)} fusion(f32[3,512,2048]{2,1,0:T(8,128)} %fusion.191, f32[3,512,2048]{2,1,0:T(8,128)} %copy-done, f32[3,512]{1,0:T(4,128)S(1)} %dynamic-slice_bitcast_fusion.2, pred[512,2048]{1,0:T(8,128)(4,1)S(1)} %broadcast_compare_fusion.5, f32[1,2048,3,64]{1,3,2,0:T(8,128)} %get-tuple-element.595, ...), kind=kOutput, calls=%fused_computation.39.clone.1 | convolution fusion | flops 437652992 | bytes 55787524 | tf_op jit(solution)/shard_map/while/body/eval_jaxpr/hqk,qhd->khd/dot_general | solution.py:242
  892.3 38.3 %all-reduce.17 = (f32[768]{0:T(1024)S(1)}, f32[768]{0:T(1024)S(1)}, f32[768]{0:T(1024)S(1)}, f32[768]{0:T(1024)S(1)}, f32[768]{0:T(1024)S(1)}, /*index=5*/f32[76...) all-reduce(bf16[768]{0:T(1024)(128)(2,1)S(1)} %get-tuple-element.37, ...), channel_id=6, replica_groups=mesh['dp'=8,'tensor'=4] {'dp'}, use_global_device_ids=true, to_apply=%region_21.22.clone | all-reduce | flops 9216 | bytes 55296
  951.0 72.5 %reduce-scatter.27.cloned.1.call-done = f32[96,768]{1,0:T(8,128)} async-done(((f32[768,768]{1,0:T(8,128)}), f32[96,768]{1,0:T(8,128)}) %reduce-scatter.27.cloned.1.call-update) | async-done | bytes 294928 | tf_op jit(solution)/shard_map/reduce_scatter | solution.py:319
  1023.5 65.9 %reduce-scatter.35.cloned.1.call-done = f32[96,192]{1,0:T(8,128)} async-done(((f32[768,192]{1,0:T(8,128)}), f32[96,192]{1,0:T(8,128)}) %reduce-scatter.35.cloned.1.call-update) | async-done | bytes 73744
  1089.4 65.4 %reduce-scatter.33.cloned.1.call-done = f32[96,192]{1,0:T(8,128)} async-done(((f32[768,192]{1,0:T(8,128)}), f32[96,192]{1,0:T(8,128)}) %reduce-scatter.33.cloned.1.call-update) | async-done | bytes 73744
  1154.8 65.9 %reduce-scatter.31.cloned.1.call-done = f32[96,192]{1,0:T(8,128)} async-done(((f32[768,192]{1,0:T(8,128)}), f32[96,192]{1,0:T(8,128)}) %reduce-scatter.31.cloned.1.call-update) | async-done | bytes 73744
  (316 shorter events, 400.5 us)
Async XLA Ops:
  8.0 84.8 %copy-start.29 = (bf16[96,192]{1,0:T(8,128)(2,1)S(1)}, bf16[96,192]{1,0:T(8,128)(2,1)}, u32[]{:S(2)}) copy-start(bf16[96,192]{1,0:T(8,128)(2,1)} %param.27) | copy-start | bytes 110596
  8.0 115.7 %copy-start.30 = (bf16[96,192]{1,0:T(8,128)(2,1)S(1)}, bf16[96,192]{1,0:T(8,128)(2,1)}, u32[]{:S(2)}) copy-start(bf16[96,192]{1,0:T(8,128)(2,1)} %param.29) | copy-start | bytes 110596
  8.1 146.8 %copy-start.31 = (bf16[96,192]{1,0:T(8,128)(2,1)S(1)}, bf16[96,192]{1,0:T(8,128)(2,1)}, u32[]{:S(2)}) copy-start(bf16[96,192]{1,0:T(8,128)(2,1)} %param.30) | copy-start | bytes 110596
  8.1 177.9 %all-gather.7.cloned.1.call-start = ((), (), s32[]{:S(2)}) async-start(), calls=%async_computation.10 | async-start | bytes 3932160 | tf_op jit(solution)/shard_map/all_gather | solution.py:108
  9.4 114.3 %copy-start.27 = (f32[512]{0:T(512)}, f32[512]{0:T(512)S(1)}, u32[]{:S(2)}) copy-start(f32[512]{0:T(512)S(1)} %broadcast_multiply_fusion.1) | copy-start | bytes 6148
  61.5 269.2 %reduce-scatter.19.cloned.1.call-start = ((), (), s32[]{:S(2)}) async-start(), calls=%async_computation.11 | async-start | bytes 3932160 | tf_op jit(solution)/shard_map/reduce_scatter | solution.py:158
  92.8 198.8 %copy-start.12 = (bf16[192,768]{0,1:T(8,128)(2,1)}, bf16[192,768]{0,1:T(8,128)(2,1)S(1)}, u32[]{:S(2)}) copy-start(bf16[192,768]{0,1:T(8,128)(2,1)S(1)} %all_gather.68) | copy-start | bytes 884740
  295.3 102.9 %all-gather.11.cloned.1.call-start = ((), (), s32[]{:S(2)}) async-start(), calls=%async_computation.13 | async-start | bytes 1327104 | tf_op jit(solution)/shard_map/all_gather | solution.py:88
  295.9 102.3 %all-gather.9.cloned.1.call-start = ((), (), s32[]{:S(2)}) async-start(), calls=%async_computation.12 | async-start | bytes 3932160 | tf_op jit(solution)/shard_map/all_gather | solution.py:163
  335.2 86.7 %all-gather.13.cloned.1.call-start = ((), (), s32[]{:S(2)}) async-start(), calls=%async_computation.14 | async-start | bytes 1327104 | tf_op jit(solution)/shard_map/all_gather | solution.py:90
  335.3 26.8 %collective-permute-start = (bf16[512,768]{1,0:T(8,128)(2,1)}, bf16[512,768]{1,0:T(8,128)(2,1)}, u32[]{:S(2)}, u32[]{:S(2)}) collective-permute-start(bf16[512,768]{1,0:T(8,128)(2,1)} %param.23), channel_id=1, source_target_pairs={{0,1},{1,2},{2,3},{3,0},{4,5},{5,6},{6,7},{7,4},{8,9},{9,10},{10,1... | collective-permute-start | bytes 2359304 | tf_op jit(solution)/shard_map/ppermute | solution.py:193
  335.8 148.8 %reduce-scatter.23.cloned.1.call-start = ((), (), s32[]{:S(2)}) async-start(), calls=%async_computation.16 | async-start | bytes 3932160 | tf_op jit(solution)/shard_map/reduce_scatter | solution.py:212
  335.8 58.2 %collective-permute-start.1 = (bf16[512,768]{1,0:T(8,128)(2,1)}, bf16[512,768]{1,0:T(8,128)(2,1)}, u32[]{:S(2)}, u32[]{:S(2)}) collective-permute-start(bf16[512,768]{1,0:T(8,128)(2,1)} %param.23), channel_id=1, source_target_pairs={{0,3},{1,0},{2,1},{3,2},{4,7},{5,4},{6,5},{7,6},{8,11},{9,8},{10,9... | collective-permute-start | bytes 2359304 | tf_op jit(solution)/shard_map/ppermute | solution.py:198
  362.0 34.1 %collective-permute-start.2 = (bf16[512,768]{1,0:T(8,128)(2,1)}, bf16[512,768]{1,0:T(8,128)(2,1)}, u32[]{:S(2)}, u32[]{:S(2)}) collective-permute-start(bf16[512,768]{1,0:T(8,128)(2,1)} %collective-permute-done), channel_id=1, source_target_pairs={{0,1},{1,2},{2,3},{3,0},{4,5},{5,6},{6,7},{7,4},{8,9},{9,10},{10,1... | collective-permute-start | bytes 2359304 | tf_op jit(solution)/shard_map/ppermute | solution.py:193
  448.1 76.8 %reduce-scatter.21.cloned.1.call-start = ((), (), s32[]{:S(2)}) async-start(), calls=%async_computation.15 | async-start | bytes 3932160 | tf_op jit(solution)/shard_map/reduce_scatter | solution.py:167
  460.1 99.7 %all-gather.15.cloned.1.call-start = ((), (), s32[]{:S(2)}) async-start(), calls=%async_computation.17 | async-start | bytes 3932160 | tf_op jit(solution)/shard_map/all_gather | solution.py:223
  531.2 335.0 %reduce-scatter.37.cloned.1.call-start = ((), (), s32[]{:S(2)}) async-start(), calls=%async_computation.24 | async-start | bytes 884736
  564.0 312.9 %reduce-scatter.25.cloned.1.call-start = ((), (), s32[]{:S(2)}) async-start(), calls=%async_computation.18 | async-start | bytes 3932160 | tf_op jit(solution)/shard_map/reduce_scatter | solution.py:272
  838.9 112.0 %reduce-scatter.29.cloned.1.call-start = ((), (), s32[]{:S(2)}) async-start(), calls=%async_computation.20 | async-start | bytes 2654208 | tf_op jit(solution)/shard_map/reduce_scatter | solution.py:320
  845.9 177.5 %reduce-scatter.27.cloned.1.call-start = ((), (), s32[]{:S(2)}) async-start(), calls=%async_computation.19 | async-start | bytes 2654208 | tf_op jit(solution)/shard_map/reduce_scatter | solution.py:319
  853.7 235.6 %reduce-scatter.35.cloned.1.call-start = ((), (), s32[]{:S(2)}) async-start(), calls=%async_computation.23 | async-start | bytes 884736
  859.9 294.9 %reduce-scatter.33.cloned.1.call-start = ((), (), s32[]{:S(2)}) async-start(), calls=%async_computation.22 | async-start | bytes 884736
  861.1 359.5 %reduce-scatter.31.cloned.1.call-start = ((), (), s32[]{:S(2)}) async-start(), calls=%async_computation.21 | async-start | bytes 884736
  863.3 72.6 %copy-start.5 = (f32[512,768]{1,0:T(8,128)S(1)}, f32[512,768]{1,0:T(8,128)}, u32[]{:S(2)}) copy-start(f32[512,768]{1,0:T(8,128)} %copy-done.4) | copy-start | bytes 4718596
  (46 other events, 803.4 us)
Sparse Core Ops, SparseCore 0:
  61.6 25.7 all-gather.6
  295.4 35.2 reduce-scatter.18
  531.3 28.5 all-gather.14
Sparse Core Ops, SparseCore 1:
  297.9 38.8 all-gather.10
  338.8 38.4 all-gather.8
  379.5 42.3 all-gather.12
  448.2 36.3 reduce-scatter.22
  487.1 37.8 reduce-scatter.20
  564.1 62.5 reduce-scatter.36
  839.0 37.8 reduce-scatter.24
  881.2 69.7 reduce-scatter.28
  955.3 68.1 reduce-scatter.26
  1027.7 61.6 reduce-scatter.34
  1093.1 61.6 reduce-scatter.32
  1159.0 61.5 reduce-scatter.30
